TPU v7x, 32 devices: a whole 2x2x4 slice. The times are simulated.
32 devices in a mesh: seq: 4 (over y, x), wshard: 8 (over z, core).
Axes of the slice: x: 2, y: 2, z: 4, core: 2. Of those that a mesh axis runs over, the one named last changes fastest.
Arguments:
- inputs: bfloat16 [8, 1024, 1024], P('wshard', 'seq'), may hold values from -6 to 6
- routes: int32 [8, 1024, 1], P('wshard', 'seq'), may hold values from 0 to 3; in each aligned block of 256 rows (0 to 255, 256 to 511, ..., all dimensions but the last counted through in order) at most 96 rows name the same one
- block_ids: int32 [8, 1024], P('wshard'), may hold values from 0 to 7, never falling along the last dimension, each value on 1 to 256 neighbouring positions
- qkv_weight: bfloat16 [1024, 3072], P('wshard'), may hold values from -0.1875 to 0.1875
- out_weight: bfloat16 [1024, 1024], P('wshard'), may hold values from -3 to 3
- gain_one: bfloat16 [1024], P('wshard'), may hold values from 0.5 to 1.5
- gain_two: bfloat16 [1024], P('wshard'), may hold values from 0.5 to 1.5
- centroid: bfloat16 [4, 1024], replicated, may hold values from -0.125 to 0.125
- up_one: bfloat16 [8, 2048, 1024], P('wshard', 'seq'), may hold values from -0.1875 to 0.1875
- down_one: bfloat16 [8, 2048, 1024], P('wshard', 'seq'), may hold values from -0.09375 to 0.09375
- up_two: bfloat16 [8, 2048, 1024], P('wshard', 'seq'), may hold values from -0.1875 to 0.1875
- down_two: bfloat16 [8, 2048, 1024], P('wshard', 'seq'), may hold values from -0.09375 to 0.09375
- cotangent: bfloat16 [8, 1024, 1024], P('wshard', 'seq'), may hold values from -6 to 6
Outputs:
- layer_out: bfloat16 [8, 1024, 1024], P('wshard', 'seq')
- input_grad: bfloat16 [8, 1024, 1024], P('wshard', 'seq')
- qkv_grad: float32 [1024, 3072], P('wshard')
- out_grad: float32 [1024, 1024], P('wshard')
- gain_one_grad: float32 [1024], P('wshard')
- gain_two_grad: float32 [1024], P('wshard')
- centroid_grad: float32 [4, 1024], replicated
- up_one_grad: float32 [8, 2048, 1024], P('wshard', 'seq')
- down_one_grad: float32 [8, 2048, 1024], P('wshard', 'seq')
- up_two_grad: float32 [8, 2048, 1024], P('wshard', 'seq')
- down_two_grad: float32 [8, 2048, 1024], P('wshard', 'seq')
Inputs may be any that keep to these rules, and one draw needn't show every extreme that they name: `routes`: among the 256 tokens of one device (aligned blocks of the flattened rows), no expert is named more than 96 times, and some device names one expert exactly 96 times. `block_ids`: along each sequence the block ids never fall, every id is used, each block spans 1 to 256 positions and one spans exactly 256.
All inputs are finite; a program needn't handle non-finite values.
Results may differ from a plain program's by a relative error of at most 0.015.
Values may be sent and summed in bfloat16 or wider, within the bound.
A program may use at most 256 MiB of HBM per device.

v0:
```python
import jax
import jax.numpy as jnp
from jax import lax
from jax.sharding import PartitionSpec as P

HEAD = 64
EPSILON = 1e-05
NEG_FILL = -1e30


def as_sent(shard):

    def short(part):
        return part.astype(jnp.bfloat16) if part.dtype == jnp.float32 else part

    return jax.tree.map(short, shard)


def from_partner(shard, axis, distance):
    return lax.ppermute(shard, axis, [(i, i ^ 1 << distance) for i in range(lax.axis_size(axis))])


def norm_rows(values, gain_vec):
    centre = jnp.mean(values, axis=-1, keepdims=True)
    shifted = values - centre
    spread = jnp.mean(shifted * shifted, axis=-1, keepdims=True)
    return shifted * lax.rsqrt(spread + EPSILON) * gain_vec


def gelu_exact(argument):
    return jax.nn.gelu(argument, approximate=False)


def gelu_back(pre_act, upstream):
    return jax.vjp(gelu_exact, pre_act)[1](upstream)[0]


def dot_rows(left_mat, right_mat):
    return lax.dot_general(
        left_mat, right_mat, (((0,), (0,)), ((), ())), preferred_element_type=jnp.float32
    )


def dot_last(left_mat, right_mat):
    return lax.dot_general(
        left_mat, right_mat, (((1,), (1,)), ((), ())), preferred_element_type=jnp.float32
    )


def heads_layout(parts_tuple):
    return jax.tree.map(
        lambda part, own: part.astype(own.dtype),
        lax.all_to_all(as_sent(parts_tuple), "seq", split_axis=1, concat_axis=0, tiled=True),
        parts_tuple,
    )


def tokens_layout(parts_tuple):
    return jax.tree.map(
        lambda part, own: part.astype(own.dtype),
        lax.all_to_all(as_sent(parts_tuple), "seq", split_axis=0, concat_axis=1, tiled=True),
        parts_tuple,
    )


def attend_forward(query_head, key_head, value_head, block_row, score_scale):
    length = query_head.shape[0]
    block_span = min(512, length)
    heads_here = query_head.shape[1] // HEAD
    keys_split = key_head.reshape(length, heads_here, HEAD)
    values_split = value_head.reshape(length, heads_here, HEAD)

    def one_block(start_row):
        query_part = lax.dynamic_slice_in_dim(query_head, start_row, block_span, 0).reshape(
            block_span, heads_here, HEAD
        )
        block_part = lax.dynamic_slice_in_dim(block_row, start_row, block_span, 0)
        scores = (
            jnp.einsum("qhc,khc->hqk", query_part, keys_split, preferred_element_type=jnp.float32)
            * score_scale
        )
        allowed = block_row[None, None, :] <= block_part[None, :, None]
        scores = jnp.where(allowed, scores, NEG_FILL)
        row_top = jnp.max(scores, axis=2, keepdims=True)
        weights = jnp.exp(scores - row_top)
        row_total = jnp.sum(weights, axis=2, keepdims=True)
        prob_low = (weights / row_total).astype(jnp.bfloat16)
        mixed_out = jnp.einsum(
            "hqk,khc->qhc", prob_low, values_split, preferred_element_type=jnp.float32
        )
        return (
            mixed_out.reshape(block_span, heads_here * HEAD).astype(jnp.bfloat16),
            (row_top + jnp.log(row_total))[:, :, 0],
        )

    starts = jnp.arange(length // block_span, dtype=jnp.int32) * block_span
    mixed_blocks, lse_blocks = lax.map(one_block, starts)
    return (
        mixed_blocks.reshape(length, heads_here * HEAD),
        jnp.transpose(lse_blocks, (1, 0, 2)).reshape(heads_here, length),
    )


def attend_backward(query_head, key_head, value_head, block_row, log_total, grad_head, score_scale):
    length = query_head.shape[0]
    block_span = min(512, length)
    heads_here = query_head.shape[1] // HEAD
    keys_split = key_head.reshape(length, heads_here, HEAD)
    values_split = value_head.reshape(length, heads_here, HEAD)

    def one_block(carry, start_row):
        key_acc, value_acc = carry
        query_part = lax.dynamic_slice_in_dim(query_head, start_row, block_span, 0).reshape(
            block_span, heads_here, HEAD
        )
        grad_part = lax.dynamic_slice_in_dim(grad_head, start_row, block_span, 0).reshape(
            block_span, heads_here, HEAD
        )
        block_part = lax.dynamic_slice_in_dim(block_row, start_row, block_span, 0)
        lse_part = lax.dynamic_slice_in_dim(log_total, start_row, block_span, 1)
        scores = (
            jnp.einsum("qhc,khc->hqk", query_part, keys_split, preferred_element_type=jnp.float32)
            * score_scale
        )
        allowed = block_row[None, None, :] <= block_part[None, :, None]
        scores = jnp.where(allowed, scores, NEG_FILL)
        prob_full = jnp.exp(scores - lse_part[:, :, None])
        prob_low = prob_full.astype(jnp.bfloat16)
        d_prob = jnp.einsum(
            "qhc,khc->hqk", grad_part, values_split, preferred_element_type=jnp.float32
        )
        row_dot = jnp.sum(prob_full * d_prob, axis=2, keepdims=True)
        d_scores = (prob_full * (d_prob - row_dot)).astype(jnp.bfloat16)
        d_query = (
            jnp.einsum("hqk,khc->qhc", d_scores, keys_split, preferred_element_type=jnp.float32)
            * score_scale
        )
        key_acc = (
            key_acc
            + jnp.einsum("hqk,qhc->khc", d_scores, query_part, preferred_element_type=jnp.float32)
            * score_scale
        )
        value_acc = value_acc + jnp.einsum(
            "hqk,qhc->khc", prob_low, grad_part, preferred_element_type=jnp.float32
        )
        return (
            (key_acc, value_acc),
            d_query.reshape(block_span, heads_here * HEAD).astype(jnp.bfloat16),
        )

    starts = jnp.arange(length // block_span, dtype=jnp.int32) * block_span
    zeros_acc = jnp.zeros((length, heads_here, HEAD), jnp.float32)
    (key_acc, value_acc), query_blocks = lax.scan(one_block, (zeros_acc, zeros_acc), starts)
    flat_width = heads_here * HEAD
    return (
        query_blocks.reshape(length, flat_width),
        key_acc.reshape(length, flat_width).astype(jnp.bfloat16),
        value_acc.reshape(length, flat_width).astype(jnp.bfloat16),
    )


def local(
    inputs,
    routes,
    block_ids,
    qkv_weight,
    out_weight,
    gain_one,
    gain_two,
    centroid,
    up_one,
    down_one,
    up_two,
    down_two,
    cotangent,
):
    tok_count = inputs.shape[1]
    model_width = inputs.shape[2]
    exp_count = centroid.shape[0]
    seq_size = lax.axis_size("seq")
    wshard_size = lax.axis_size("wshard")
    slots = max(1, 9 * tok_count // (8 * exp_count))
    score_scale = HEAD ** (-0.5)
    head_width = model_width // seq_size
    seq_index = lax.axis_index("seq")
    same_core = [list(range(core, wshard_size, 2)) for core in range(2)]
    qkv_parts = qkv_weight.reshape(-1, 3, model_width)
    qkv_own = lax.dynamic_slice_in_dim(qkv_parts, seq_index * head_width, head_width, 2)
    qkv_heads = lax.all_gather(qkv_own.reshape(-1, 3 * head_width), "wshard", axis=0, tiled=True)
    full_gain_one = lax.all_gather(gain_one, "wshard", axis=0, tiled=True)
    full_gain_two = lax.all_gather(gain_two, "wshard", axis=0, tiled=True)
    gain_first = full_gain_one.astype(jnp.float32)
    gain_second = full_gain_two.astype(jnp.float32)
    tokens_in = inputs[0].astype(jnp.float32)
    normed_one = norm_rows(tokens_in, gain_first).astype(jnp.bfloat16)
    normed_all = lax.all_gather(normed_one, "seq", axis=0, tiled=True)
    full_out = lax.all_gather(out_weight, "wshard", axis=0, tiled=True)
    up_a, down_a, up_b, down_b = (
        lax.all_gather(part[0], "seq", axis=0, tiled=True)
        for part in (up_one, down_one, up_two, down_two)
    )
    projected = jnp.dot(normed_all, qkv_heads, preferred_element_type=jnp.float32).astype(
        jnp.bfloat16
    )
    query_head = projected[:, :head_width]
    key_head = projected[:, head_width : 2 * head_width]
    value_head = projected[:, 2 * head_width :]
    block_row = block_ids[0]
    mixed_head, log_total = attend_forward(query_head, key_head, value_head, block_row, score_scale)
    (mixed_tok,) = tokens_layout((mixed_head,))
    hidden = tokens_in + jnp.dot(mixed_tok, full_out, preferred_element_type=jnp.float32)
    normed_two = norm_rows(hidden, gain_second).astype(jnp.bfloat16)
    route_ids = routes[0, :, 0]
    expert_ids = jnp.arange(exp_count, dtype=jnp.int32)
    expert_hot = route_ids[:, None] == expert_ids[None, :]
    hot_low = expert_hot.astype(jnp.bfloat16)
    logits = dot_last(normed_two, centroid)
    chosen = jnp.sum(jnp.where(expert_hot, logits, 0.0), axis=1)
    sigmoid_val = jax.nn.sigmoid(chosen)
    positions = jnp.arange(tok_count, dtype=jnp.int32)
    lower_tri = (positions[:, None] >= positions[None, :]).astype(jnp.bfloat16)
    running = jnp.dot(lower_tri, hot_low, preferred_element_type=jnp.float32)
    local_rank = (jnp.sum(jnp.where(expert_hot, running, 0.0), axis=1) - 1.0).astype(jnp.int32)
    kept_mask = local_rank < slots
    gate_val = jnp.where(kept_mask, sigmoid_val, 0.0)
    slot_id = route_ids * slots + local_rank
    slot_ids = jnp.arange(exp_count * slots, dtype=jnp.int32)
    dispatch = ((slot_ids[:, None] == slot_id[None, :]) & kept_mask[None, :]).astype(jnp.bfloat16)
    dy_rows = cotangent[0].astype(jnp.float32)

    def exchange(slab):
        return lax.all_to_all(
            slab, "wshard", split_axis=0, concat_axis=0, axis_index_groups=same_core, tiled=True
        )

    both = jnp.concatenate((normed_two, (gate_val[:, None] * dy_rows).astype(jnp.bfloat16)), axis=1)
    packed = jnp.dot(dispatch, both, preferred_element_type=jnp.float32).astype(jnp.bfloat16)
    own_both = exchange(packed.reshape(exp_count, slots, 2 * model_width)).reshape(
        exp_count * slots, 2 * model_width
    )
    pair_both = from_partner(own_both, "wshard", 0)
    sent_all = jnp.concatenate((own_both[:, :model_width], pair_both[:, :model_width]), axis=0)
    d_second_all = jnp.concatenate((own_both[:, model_width:], pair_both[:, model_width:]), axis=0)
    own_rows = exp_count * slots

    def pair_total(partial_sum):
        other = from_partner(partial_sum, "wshard", 0)
        return partial_sum + jnp.concatenate((other[own_rows:], other[:own_rows]), axis=0)

    def add_rows(base, term):
        return (base.astype(jnp.float32) + term).astype(jnp.bfloat16)

    pre_one = dot_last(sent_all, up_a)
    act_one = gelu_exact(pre_one).astype(jnp.bfloat16)
    first_all = add_rows(
        sent_all, pair_total(jnp.dot(act_one, down_a, preferred_element_type=jnp.float32))
    )
    pre_two = dot_last(first_all, up_b)
    act_two = gelu_exact(pre_two).astype(jnp.bfloat16)
    second_part = jnp.dot(act_two, down_b, preferred_element_type=jnp.float32)
    second_own = add_rows(
        first_all[:own_rows],
        second_part[:own_rows] + from_partner(second_part[own_rows:], "wshard", 0),
    )
    d_pre_two = gelu_back(pre_two, dot_last(d_second_all, down_b)).astype(jnp.bfloat16)
    d_first_all = add_rows(
        d_second_all, pair_total(jnp.dot(d_pre_two, up_b, preferred_element_type=jnp.float32))
    )
    d_pre_one = gelu_back(pre_one, dot_last(d_first_all, down_a)).astype(jnp.bfloat16)
    d_sent_part = jnp.dot(d_pre_one, up_a, preferred_element_type=jnp.float32)
    d_sent_own = add_rows(
        d_first_all[:own_rows],
        d_sent_part[:own_rows] + from_partner(d_sent_part[own_rows:], "wshard", 0),
    )

    def weight_grad(left, right):
        return lax.psum_scatter(
            dot_rows(left, right).astype(jnp.bfloat16), "seq", scatter_dimension=0, tiled=True
        ).astype(jnp.float32)

    grad_down_b = weight_grad(act_two, d_second_all)
    grad_up_b = weight_grad(d_pre_two, first_all)
    grad_down_a = weight_grad(act_one, d_first_all)
    grad_up_a = weight_grad(d_pre_one, sent_all)

    def give_back(rows):
        return dot_rows(
            dispatch,
            exchange(rows.reshape(exp_count, slots, model_width)).reshape(own_rows, model_width),
        )

    returned_tok = give_back(second_own)
    layer_out = (hidden + gate_val[:, None] * returned_tok).astype(jnp.bfloat16)
    d_gate = jnp.where(kept_mask, jnp.sum(dy_rows * returned_tok, axis=1), 0.0)
    d_chosen = d_gate * sigmoid_val * (1.0 - sigmoid_val)
    d_sent_tok = give_back(d_sent_own)
    centroid_tok = jnp.dot(hot_low, centroid, preferred_element_type=jnp.float32)
    d_normed_two = d_sent_tok + d_chosen[:, None] * centroid_tok
    centroid_term = lax.dot_general(
        expert_hot.astype(jnp.float32),
        d_chosen[:, None] * normed_two.astype(jnp.float32),
        (((0,), (0,)), ((), ())),
        precision=lax.Precision.HIGHEST,
        preferred_element_type=jnp.float32,
    )
    norm_two_back = jax.vjp(norm_rows, hidden, gain_second)[1]
    d_hidden_norm, d_gain_second = norm_two_back(d_normed_two)
    d_hidden = dy_rows + d_hidden_norm
    d_branch = d_hidden.astype(jnp.bfloat16)
    grad_out_full = dot_rows(mixed_tok, d_branch)
    d_mixed = dot_last(d_branch, full_out).astype(jnp.bfloat16)
    (d_mixed_head,) = heads_layout((d_mixed,))
    d_query, d_key, d_value = attend_backward(
        query_head, key_head, value_head, block_row, log_total, d_mixed_head, score_scale
    )
    d_projected = jnp.concatenate((d_query, d_key, d_value), axis=1)
    grad_qkv_heads = dot_rows(normed_all, d_projected)
    d_normed_part = dot_last(d_projected, qkv_heads)
    d_normed_one = lax.psum_scatter(
        d_normed_part.astype(jnp.bfloat16), "seq", scatter_dimension=0, tiled=True
    ).astype(jnp.float32)
    norm_one_back = jax.vjp(norm_rows, tokens_in, gain_first)[1]
    d_tokens_norm, d_gain_first = norm_one_back(d_normed_one)
    input_grad = (d_hidden + d_tokens_norm).astype(jnp.bfloat16)
    qkv_sum = lax.psum_scatter(grad_qkv_heads, "wshard", scatter_dimension=0, tiled=True)
    qkv_all = lax.all_gather(qkv_sum.astype(jnp.bfloat16), "seq", axis=0, tiled=False)
    qkv_rows = qkv_sum.shape[0]
    grad_qkv = (
        jnp.transpose(qkv_all.reshape(seq_size, qkv_rows, 3, head_width), (1, 2, 0, 3))
        .reshape(qkv_rows, 3 * model_width)
        .astype(jnp.float32)
    )
    out_part = lax.psum_scatter(grad_out_full, "wshard", scatter_dimension=0, tiled=True)
    grad_out = lax.psum(out_part.astype(jnp.bfloat16), "seq").astype(jnp.float32)
    small = jnp.concatenate((d_gain_first[None], d_gain_second[None], centroid_term), axis=0)
    small = lax.psum(small, ("seq", "wshard"))
    gain_rows = gain_one.shape[0]
    gain_at = lax.axis_index("wshard") * gain_rows
    grad_gain_one = lax.dynamic_slice_in_dim(small[0], gain_at, gain_rows, 0)
    grad_gain_two = lax.dynamic_slice_in_dim(small[1], gain_at, gain_rows, 0)
    grad_centroid = small[2:]
    return (
        layer_out[None],
        input_grad[None],
        grad_qkv,
        grad_out,
        grad_gain_one,
        grad_gain_two,
        grad_centroid,
        grad_up_a[None],
        grad_down_a[None],
        grad_up_b[None],
        grad_down_b[None],
    )


def solution(mesh):
    return jax.shard_map(
        local,
        mesh=mesh,
        in_specs=(
            P("wshard", "seq", None),
            P("wshard", "seq", None),
            P("wshard", None),
            P("wshard", None),
            P("wshard", None),
            P("wshard"),
            P("wshard"),
            P(),
            P("wshard", "seq", None),
            P("wshard", "seq", None),
            P("wshard", "seq", None),
            P("wshard", "seq", None),
            P("wshard", "seq", None),
        ),
        out_specs=(
            P("wshard", "seq", None),
            P("wshard", "seq", None),
            P("wshard", None),
            P("wshard", None),
            P("wshard"),
            P("wshard"),
            P(),
            P("wshard", "seq", None),
            P("wshard", "seq", None),
            P("wshard", "seq", None),
            P("wshard", "seq", None),
        ),
        check_vma=False,
    )
```

profile of v0, /device:TPU:0, one launch (start us, length us, event | category | flops | bytes accessed | tf_op | source)
XLA Modules:
  0.0 793.7 jit_solution(11065188266168961729)
XLA Ops:
  9.5 13.6 %all-gather.5 = bf16[8,1,128]{2,1,0:T(2,128)(2,1)S(1)} all-gather(bf16[1,1,128]{2,1,0:T(2,128)(2,1)} %bitcast.284), channel_id=1, replica_groups=mesh['seq'=4,'wshard'=8] {'wshard'}, dimensions={0}, use_global_device_ids=true | all-gather | bytes 2304 | tf_op jit(solution)/shard_map/all_gather | solution.py:190
  31.4 8.6 %all-gather.17.cloned.1.call-done = bf16[1024,768]{0,1:T(8,128)(2,1)} async-done(((bf16[128,768]{0,1:T(8,128)(2,1)}), bf16[1024,768]{0,1:T(8,128)(2,1)}) %all-gather.17.cloned.1.call-update) | async-done | bytes 1572880 | tf_op jit(solution)/shard_map/all_gather | solution.py:189
  40.0 36.4 %all-gather.15.cloned.1.call-done = bf16[1024,1024]{1,0:T(8,128)(2,1)} async-done(((bf16[256,1024]{1,0:T(8,128)(2,1)}), bf16[1024,1024]{1,0:T(8,128)(2,1)}) %all-gather.15.cloned.1.call-update) | async-done | bytes 2097168 | tf_op jit(solution)/shard_map/all_gather | solution.py:196
  76.4 3.9 convolution_convert_fusion.6
  82.1 24.5 %while.27 = (s32[]{:T(128)}, bf16[2,512,256]{2,1,0:T(8,128)(2,1)}, f32[2,4,512]{2,1,0:T(4,128)S(1)}, s32[1,1024]{1,0:T(1,128)S(1)}, s32[2]{0:T(128)S(1)}, /*inde...) while((s32[]{:T(128)}, bf16[2,512,256]{2,1,0:T(8,128)(2,1)}, ...), condition=%wide.region_5.6_spmd, body=%wide.region_2.5_spmd.sunk | while | flops 562690048 | bytes 30485168 | solution.py:97
  87.9 2.4 fusion.188
  90.3 3.1 fusion.189
  100.1 2.4 fusion.188
  102.5 3.1 fusion.189
  106.5 3.6 all-to-all-start
  110.2 11.7 %all-gather.6 = bf16[8,1,128]{2,1,0:T(2,128)(2,1)S(1)} all-gather(bf16[1,1,128]{2,1,0:T(2,128)(2,1)S(1)} %bitcast.285), channel_id=1, replica_groups=mesh['seq'=4,'wshard'=8] {'wshard'}, dimensions={0}, use_global_device_ids=true | all-gather | bytes 2304 | tf_op jit(solution)/shard_map/all_gather | solution.py:191
  122.5 2.6 fusion.122
  127.2 31.7 %all_to_all.53 = bf16[4,72,2048]{2,1,0:T(8,128)(2,1)S(1)} all-to-all(bf16[4,72,2048]{2,1,0:T(8,128)(2,1)S(1)} %bitcast.260), channel_id=1, replica_groups={{0,2,4,6},{1,3,5,7},{8,10,12,14},{9,11,13,15},{16,18,20,22},{17,19,21,2..., dimensions={0} | all-to-all | bytes 2359296 | tf_op jit(solution)/shard_map/all_to_all | solution.py:232
  162.0 16.9 %multiply_convert_fusion.2 = (bf16[576,2048]{1,0:T(8,128)(2,1)}, f32[576,2048]{1,0:T(8,128)}, f32[576,2048]{1,0:T(8,128)}) fusion(bf16[1,2048,1024]{2,1,0:T(8,128)(2,1)} %all-gather.21.cloned.1.call-done, bf16[288,1024]{1,0:T(8,128)(2,1)S(1)} %get-tuple-element.269, bf16[288,1024]{1,0:T(8,128)(2,1)S(1)} %get-tuple-element.267), kind=kOutput, calls=%fused_computation.52 | convolution fusion | flops 2494955520 | bytes 17170432 | tf_op jit(solution)/shard_map/dot_general | solution.py:45
  178.8 36.5 %all-gather.23.cloned.1.call-done = bf16[1,2048,1024]{2,1,0:T(8,128)(2,1)} async-done(((bf16[1,512,1024]{2,1,0:T(8,128)(2,1)}), bf16[1,2048,1024]{2,1,0:T(8,128)(2,1)}) %all-gather.23.cloned.1.call-update) | async-done | bytes 4194320 | tf_op jit(solution)/shard_map/all_gather | solution.py:199
  215.3 5.1 fusion.43
  220.5 4.5 collective-permute-done.1
  226.1 43.5 %all-gather.25.cloned.1.call-done = bf16[1,2048,1024]{2,1,0:T(8,128)(2,1)} async-done(((bf16[1,512,1024]{2,1,0:T(8,128)(2,1)}), bf16[1,2048,1024]{2,1,0:T(8,128)(2,1)}) %all-gather.25.cloned.1.call-update) | async-done | bytes 4194320 | tf_op jit(solution)/shard_map/all_gather | solution.py:199
  269.6 16.8 %multiply_convert_fusion.1 = (bf16[576,2048]{1,0:T(8,128)(2,1)}, f32[576,2048]{1,0:T(8,128)}, f32[576,2048]{1,0:T(8,128)}) fusion(bf16[576,1024]{1,0:T(8,128)(2,1)S(1)} %fusion.54, bf16[1,2048,1024]{2,1,0:T(8,128)(2,1)} %all-gather.25.cloned.1.call-done), kind=kOutput, calls=%fused_computation.39 | convolution fusion | flops 2492596224 | bytes 17170432 | tf_op jit(solution)/shard_map/dot_general | solution.py:45
  286.4 37.7 %all-gather.27.cloned.1.call-done = bf16[1,2048,1024]{2,1,0:T(8,128)(2,1)} async-done(((bf16[1,512,1024]{2,1,0:T(8,128)(2,1)}), bf16[1,2048,1024]{2,1,0:T(8,128)(2,1)}) %all-gather.27.cloned.1.call-update) | async-done | bytes 4194320 | tf_op jit(solution)/shard_map/all_gather | solution.py:199
  324.1 8.6 %add_convert_fusion.1 = bf16[576,2048]{1,0:T(8,128)(2,1)S(1)} fusion(f32[576,2048]{1,0:T(8,128)} %get-tuple-element.250, f32[576,2048]{1,0:T(8,128)} %get-tuple-element.276, bf16[1,2048,1024]{2,1,0:T(8,128)(2,1)} %all-gather.27.cloned.1.call-done, bf16[288,1024]{1,0:T(8,128)(2,1)S(1)} %get-tuple-element.268, bf16[288,1024]{1,0:T(8,128)(2,1)S(1)} %copy-done.26), kind=kOutput, calls=%fused_computation.38 | convolution fusion | flops 2434793472 | bytes 17170432 | tf_op jit(solution)/shard_map/dot_general | solution.py:45
  332.7 4.1 fusion.37
  336.8 5.1 convolution_convert_fusion.1
  341.9 5.3 fusion.35
  347.9 2.4 fusion.116
  350.3 2.4 fusion.56
  353.2 6.8 add_convert_fusion
  360.1 2.6 fusion.45
  365.1 4.6 all-to-all-start.2
  369.7 2.9 fusion.65
  372.6 13.6 %all-to-all-done.2 = bf16[4,72,1024]{2,1,0:T(8,128)(2,1)S(1)} async-done(((bf16[4,72,1024]{2,1,0:T(8,128)(2,1)}), bf16[4,72,1024]{2,1,0:T(8,128)(2,1)S(1)}, u32[]{:S(2)}, u32[]{:S(2)}) %all-to-all-start.2) | async-done | bytes 589856 | tf_op jit(solution)/shard_map/all_to_all | solution.py:232
  387.0 4.2 all-to-all-start.3
  391.2 2.5 fusion.75
  395.1 11.7 %all-to-all-done.3 = bf16[4,72,1024]{2,1,0:T(8,128)(2,1)} async-done(((bf16[4,72,1024]{2,1,0:T(8,128)(2,1)}), bf16[4,72,1024]{2,1,0:T(8,128)(2,1)}, u32[]{:S(2)}, u32[]{:S(2)}) %all-to-all-start.3) | async-done | bytes 589856 | tf_op jit(solution)/shard_map/all_to_all | solution.py:232
  409.2 2.5 fusion.113
  414.5 4.1 all-to-all-start.4
  418.7 6.9 convolution_convert_fusion
  427.1 64.5 %while.28 = (s32[]{:T(128)}, f32[1024,4,64]{0,2,1:T(8,128)S(1)}, f32[1024,4,64]{0,2,1:T(8,128)}, bf16[2,512,256]{2,1,0:T(8,128)(2,1)}, s32[2]{0:T(128)S(1)}, /*i...) while((s32[]{:T(128)}, f32[1024,4,64]{0,2,1:T(8,128)S(1)}, ...), condition=%wide.region_15.16_spmd.clone, body=%wide.region_13.15_spmd.clone.sunk | while | flops 1375729664 | bytes 118819648 | solution.py:153
  431.0 4.6 fusion.200
  437.3 6.1 multiply_reduce_fusion.5
  443.8 2.4 multiply_convert_fusion.5
  450.5 3.2 fusion.201
  453.7 5.9 fusion.202
  463.3 4.6 fusion.200
  469.6 5.8 multiply_reduce_fusion.5
  482.3 3.1 fusion.201
  485.5 6.2 fusion.202
  493.7 4.7 convolution_convert_fusion.5
  498.5 6.9 convolution_convert_fusion.3
  506.5 2.7 fusion.124
  509.3 7.1 convolution_convert_fusion.2
  516.5 5.3 fusion.84
  522.6 2.8 bitcast_convert_fusion.1
  525.4 2.8 bitcast_convert_fusion
  528.2 5.0 reduce-scatter.8.cloned.1.call-done
  536.3 39.9 %psum.15 = f32[6,1024]{1,0:T(8,128)S(1)} all-reduce(f32[6,1024]{1,0:T(8,128)S(1)} %pad_maximum_fusion.9), channel_id=1, replica_groups=mesh['seq'=4,'wshard'=8] {'seq','wshard'}, use_global_device_ids=true, to_apply=%region_24.25 | all-reduce | flops 6144 | bytes 49152 | tf_op jit(solution)/shard_map/psum | solution.py:336
  579.7 9.5 %reduce-scatter.14.cloned.1.call-done = bf16[512,1024]{1,0:T(8,128)(2,1)} async-done(((bf16[2048,1024]{1,0:T(8,128)(2,1)}), bf16[512,1024]{1,0:T(8,128)(2,1)}) %reduce-scatter.14.cloned.1.call-update) | async-done | bytes 1048592 | tf_op jit(solution)/shard_map/reduce_scatter | solution.py:277
  589.2 2.8 bitcast_convert_fusion.3
  592.0 49.5 %reduce-scatter.12.cloned.1.call-done = f32[128,1024]{1,0:T(8,128)} async-done(((f32[1024,1024]{1,0:T(8,128)}), f32[128,1024]{1,0:T(8,128)}) %reduce-scatter.12.cloned.1.call-update) | async-done | bytes 524304 | tf_op jit(solution)/shard_map/reduce_scatter | solution.py:333
  643.3 52.3 %reduce-scatter.16.cloned.1.call-done = bf16[512,1024]{1,0:T(8,128)(2,1)} async-done(((bf16[2048,1024]{1,0:T(8,128)(2,1)}), bf16[512,1024]{1,0:T(8,128)(2,1)}) %reduce-scatter.16.cloned.1.call-update) | async-done | bytes 1048592 | tf_op jit(solution)/shard_map/reduce_scatter | solution.py:277
  695.5 2.8 bitcast_convert_fusion.2
  698.3 39.8 %reduce-scatter.10.cloned.1.call-done = f32[128,768]{1,0:T(8,128)} async-done(((f32[1024,768]{1,0:T(8,128)}), f32[128,768]{1,0:T(8,128)}) %reduce-scatter.10.cloned.1.call-update) | async-done | bytes 393232 | tf_op jit(solution)/shard_map/reduce_scatter | solution.py:325
  739.1 12.5 %all-gather.4 = bf16[512,768]{1,0:T(8,128)(2,1)S(1)} all-gather(bf16[128,768]{1,0:T(8,128)(2,1)S(1)} %convert_element_type.235), channel_id=6, replica_groups=mesh['seq'=4,'wshard'=8] {'seq'}, dimensions={0}, use_global_device_ids=true | all-gather | bytes 983040 | tf_op jit(solution)/shard_map/all_gather | solution.py:326
  754.3 30.7 %all-reduce.2.cloned.1.call-done = bf16[128,1024]{1,0:T(8,128)(2,1)} async-done(((bf16[128,1024]{1,0:T(8,128)(2,1)}), bf16[128,1024]{1,0:T(8,128)(2,1)}) %all-reduce.2.cloned.1.call-update) | async-done | bytes 262160 | tf_op jit(solution)/shard_map/psum | solution.py:334
  (309 shorter events, 76.4 us)
Async XLA Ops:
  7.2 119.0 %copy-start = (bf16[4,1024]{1,0:T(4,128)(2,1)S(1)}, bf16[4,1024]{1,0:T(4,128)(2,1)}, u32[]{:S(2)}) copy-start(bf16[4,1024]{1,0:T(4,128)(2,1)} %param.24) | copy-start | bytes 24580
  7.2 32.8 %all-gather.17.cloned.1.call-start = ((), (), s32[]{:S(2)}) async-start(), calls=%async_computation.13 | async-start | bytes 1769472 | tf_op jit(solution)/shard_map/all_gather | solution.py:189
  9.5 67.0 %all-gather.15.cloned.1.call-start = ((), (), s32[]{:S(2)}) async-start(), calls=%async_computation.12 | async-start | bytes 2621440 | tf_op jit(solution)/shard_map/all_gather | solution.py:196
  28.9 93.5 %all-gather.19.cloned.1.call-start = ((), (), s32[]{:S(2)}) async-start(), calls=%async_computation.14 | async-start | bytes 2359296 | tf_op jit(solution)/shard_map/all_gather | solution.py:197
  29.6 132.3 %all-gather.21.cloned.1.call-start = ((), (), s32[]{:S(2)}) async-start(), calls=%async_computation.23 | async-start | bytes 5242880 | tf_op jit(solution)/shard_map/all_gather | solution.py:199
  30.2 185.1 %all-gather.23.cloned.1.call-start = ((), (), s32[]{:S(2)}) async-start(), calls=%async_computation.24 | async-start | bytes 5242880 | tf_op jit(solution)/shard_map/all_gather | solution.py:199
  30.8 238.8 %all-gather.25.cloned.1.call-start = ((), (), s32[]{:S(2)}) async-start(), calls=%async_computation.25 | async-start | bytes 5242880 | tf_op jit(solution)/shard_map/all_gather | solution.py:199
  31.4 50.6 %copy-start.34 = (s32[1,1024]{1,0:T(1,128)S(1)}, s32[1,1024]{1,0:T(1,128)}, u32[]{:S(2)}) copy-start(s32[1,1024]{1,0:T(1,128)} %param.19) | copy-start | bytes 12292
  82.0 28.2 %copy-start.68 = (bf16[128]{0:T(256)(128)(2,1)S(1)}, bf16[128]{0:T(256)(128)(2,1)}, u32[]{:S(2)}) copy-start(bf16[128]{0:T(256)(128)(2,1)} %param.23) | copy-start | bytes 772
  82.1 39.9 %copy-start.50 = (s32[1,256,1]{1,2,0:T(1,128)S(1)}, s32[1,256,1]{1,2,0:T(1,128)}, u32[]{:S(2)}) copy-start(s32[1,256,1]{1,2,0:T(1,128)} %param.18) | copy-start | bytes 3076
  82.1 40.4 %copy-start.6 = (bf16[1,256,1024]{2,1,0:T(8,128)(2,1)S(1)}, bf16[1,256,1024]{2,1,0:T(8,128)(2,1)}, u32[]{:S(2)}) copy-start(bf16[1,256,1024]{2,1,0:T(8,128)(2,1)} %param.17) | copy-start | bytes 1572868
  106.5 15.7 %copy-start.42 = (f32[2,4,512]{2,1,0:T(4,128)}, f32[2,4,512]{2,1,0:T(4,128)S(1)}, u32[]{:S(2)}) copy-start(f32[2,4,512]{2,1,0:T(4,128)S(1)} %get-tuple-element.124) | copy-start | bytes 49156
  106.5 15.7 %copy-start.72 = (s32[2]{0:T(128)}, s32[2]{0:T(128)S(1)}, u32[]{:S(2)}) copy-start(s32[2]{0:T(128)S(1)} %get-tuple-element.586) | copy-start | bytes 28
  106.5 19.9 %copy-start.2 = (bf16[1024,4,64]{0,2,1:T(8,128)(2,1)}, bf16[1024,4,64]{0,2,1:T(8,128)(2,1)S(1)}, u32[]{:S(2)}) copy-start(bf16[1024,4,64]{0,2,1:T(8,128)(2,1)S(1)} %get-tuple-element.514) | copy-start | bytes 1572868
  106.5 19.9 %copy-start.8 = (bf16[1024,4,64]{0,2,1:T(8,128)(2,1)}, bf16[1024,4,64]{0,2,1:T(8,128)(2,1)S(1)}, u32[]{:S(2)}) copy-start(bf16[1024,4,64]{0,2,1:T(8,128)(2,1)S(1)} %get-tuple-element.517) | copy-start | bytes 1572868
  106.5 20.0 %copy-start.13 = (bf16[1,256,1024]{2,1,0:T(8,128)(2,1)S(1)}, bf16[1,256,1024]{2,1,0:T(8,128)(2,1)}, u32[]{:S(2)}) copy-start(bf16[1,256,1024]{2,1,0:T(8,128)(2,1)} %param.29) | copy-start | bytes 1572868
  106.5 15.6 %all-to-all-start = ((bf16[4,256,256]{2,1,0:T(8,128)(2,1)}), bf16[4,256,256]{2,1,0:T(8,128)(2,1)S(1)}, u32[]{:S(2)}, u32[]{:S(2)}) async-start(bf16[4,256,256]{2,1,0:T(8,128)(2,1)} %bitcast.14), calls=%async_computation | async-start | bytes 1048576 | tf_op jit(solution)/shard_map/all_to_all | solution.py:61
  110.2 213.9 %all-gather.27.cloned.1.call-start = ((), (), s32[]{:S(2)}) async-start(), calls=%async_computation.26 | async-start | bytes 5242880 | tf_op jit(solution)/shard_map/all_gather | solution.py:199
  125.0 33.9 %copy-start.48 = (f32[256]{0:T(256)}, f32[256]{0:T(256)S(1)}, u32[]{:S(2)}) copy-start(f32[256]{0:T(256)S(1)} %broadcast_multiply_fusion) | copy-start | bytes 3076
  125.3 34.8 %copy-start.54 = (f32[256]{0:T(256)}, f32[256]{0:T(256)S(1)}, u32[]{:S(2)}) copy-start(f32[256]{0:T(256)S(1)} %fusion.103) | copy-start | bytes 3076
  126.4 35.4 %copy-start.58 = (f32[256]{0:T(256)}, f32[256]{0:T(256)S(1)}, u32[]{:S(2)}) copy-start(f32[256]{0:T(256)S(1)} %fusion.68) | copy-start | bytes 3076
  126.5 32.5 %copy-start.64 = (f32[256]{0:T(256)}, f32[256]{0:T(256)S(1)}, u32[]{:S(2)}) copy-start(f32[256]{0:T(256)S(1)} %get-tuple-element.253) | copy-start | bytes 3076
  126.5 35.4 %copy-start.66 = (pred[256]{0:T(512)(128)(4,1)}, pred[256]{0:T(512)(128)(4,1)S(1)}, u32[]{:S(2)}) copy-start(pred[256]{0:T(512)(128)(4,1)S(1)} %get-tuple-element.254) | copy-start | bytes 772
  158.9 2.8 collective-permute-start
  159.0 363.6 %reduce-scatter.18.cloned.1.call-start = ((), (), s32[]{:S(2)}) async-start(), calls=%async_computation.21 | async-start | bytes 5242880 | tf_op jit(solution)/shard_map/reduce_scatter | solution.py:277
  160.2 65.1 %copy-start.22 = (bf16[288,1024]{1,0:T(8,128)(2,1)}, bf16[288,1024]{1,0:T(8,128)(2,1)S(1)}, u32[]{:S(2)}) copy-start(bf16[288,1024]{1,0:T(8,128)(2,1)S(1)} %get-tuple-element.267) | copy-start | bytes 1769476
  161.9 63.4 %copy-start.24 = (bf16[288,1024]{1,0:T(8,128)(2,1)}, bf16[288,1024]{1,0:T(8,128)(2,1)S(1)}, u32[]{:S(2)}) copy-start(bf16[288,1024]{1,0:T(8,128)(2,1)S(1)} %get-tuple-element.269) | copy-start | bytes 1769476
  161.9 188.4 %copy-start.27 = (bf16[288,1024]{1,0:T(8,128)(2,1)}, bf16[288,1024]{1,0:T(8,128)(2,1)S(1)}, u32[]{:S(2)}) copy-start(bf16[288,1024]{1,0:T(8,128)(2,1)S(1)} %get-tuple-element.268) | copy-start | bytes 1769476
  220.4 4.6 collective-permute-start.1
  226.1 98.0 %copy-start.26 = (bf16[288,1024]{1,0:T(8,128)(2,1)S(1)}, bf16[288,1024]{1,0:T(8,128)(2,1)}, u32[]{:S(2)}) copy-start(bf16[288,1024]{1,0:T(8,128)(2,1)} %get-tuple-element.266) | copy-start | bytes 1769476
  324.0 8.6 %copy-start.71 = (bf16[1,2048,1024]{2,1,0:T(8,128)(2,1)S(1)}, bf16[1,2048,1024]{2,1,0:T(8,128)(2,1)}, u32[]{:S(2)}) copy-start(bf16[1,2048,1024]{2,1,0:T(8,128)(2,1)} %all-gather.25.cloned.1.call-done) | copy-start | bytes 12582916
  336.8 11.1 %collective-permute-start.3 = (f32[576,1024]{1,0:T(8,128)}, f32[576,1024]{1,0:T(8,128)}, u32[]{:S(2)}, u32[]{:S(2)}) collective-permute-start(f32[576,1024]{1,0:T(8,128)} %fusion.37), channel_id=1, source_target_pairs={{0,1},{1,0},{2,3},{3,2},{4,5},{5,4},{6,7},{7,6},{8,9},{9,8},{10,11... | collective-permute-start | bytes 7077896 | tf_op jit(solution)/shard_map/ppermute | solution.py:20
  347.3 16.6 %collective-permute-start.2 = (f32[288,1024]{1,0:T(8,128)S(1)}, f32[288,1024]{1,0:T(8,128)S(1)}, u32[]{:S(2)}, u32[]{:S(2)}) collective-permute-start(f32[288,1024]{1,0:T(8,128)S(1)} %slice.89), channel_id=1, source_target_pairs={{0,1},{1,0},{2,3},{3,2},{4,5},{5,4},{6,7},{7,6},{8,9},{9,8},{10,11... | collective-permute-start | bytes 3538952 | tf_op jit(solution)/shard_map/ppermute | solution.py:20
  352.8 7.3 copy-start.20
  363.9 27.2 %copy-start.14 = (bf16[1,256,1024]{2,1,0:T(8,128)(2,1)S(1)}, bf16[1,256,1024]{2,1,0:T(8,128)(2,1)}, u32[]{:S(2)}) copy-start(bf16[1,256,1024]{2,1,0:T(8,128)(2,1)} %param.29) | copy-start | bytes 1572868
  363.9 27.3 %copy-start.57 = (s32[256]{0:T(256)S(1)}, s32[256]{0:T(256)}, u32[]{:S(2)}) copy-start(s32[256]{0:T(256)} %copy-done.56) | copy-start | bytes 3076
  363.9 27.3 %copy-start.67 = (pred[256]{0:T(512)(128)(4,1)S(1)}, pred[256]{0:T(512)(128)(4,1)}, u32[]{:S(2)}) copy-start(pred[256]{0:T(512)(128)(4,1)} %copy-done.66) | copy-start | bytes 772
  363.9 5.8 collective-permute-start.4
  365.1 28.6 %copy-start.59 = (f32[256]{0:T(256)S(1)}, f32[256]{0:T(256)}, u32[]{:S(2)}) copy-start(f32[256]{0:T(256)} %copy-done.58) | copy-start | bytes 3076
  365.1 28.6 %copy-start.51 = (s32[1,256,1]{1,2,0:T(1,128)S(1)}, s32[1,256,1]{1,2,0:T(1,128)}, u32[]{:S(2)}) copy-start(s32[1,256,1]{1,2,0:T(1,128)} %param.18) | copy-start | bytes 3076
  365.1 41.7 %copy-start.5 = (f32[256,1024]{1,0:T(8,128)S(1)}, f32[256,1024]{1,0:T(8,128)}, u32[]{:S(2)}) copy-start(f32[256,1024]{1,0:T(8,128)} %copy-done.4) | copy-start | bytes 3145732
  365.1 41.7 %copy-start.45 = (f32[8,1,128]{2,1,0:T(1,128)S(1)}, f32[8,1,128]{2,1,0:T(1,128)}, u32[]{:S(2)}) copy-start(f32[8,1,128]{2,1,0:T(1,128)} %copy-done.44) | copy-start | bytes 12292
  365.1 41.7 %copy-start.49 = (f32[256]{0:T(256)S(1)}, f32[256]{0:T(256)}, u32[]{:S(2)}) copy-start(f32[256]{0:T(256)} %copy-done.48) | copy-start | bytes 3076
  365.1 41.7 %copy-start.55 = (f32[256]{0:T(256)S(1)}, f32[256]{0:T(256)}, u32[]{:S(2)}) copy-start(f32[256]{0:T(256)} %copy-done.54) | copy-start | bytes 3076
  365.1 21.0 %all-to-all-start.2 = ((bf16[4,72,1024]{2,1,0:T(8,128)(2,1)}), bf16[4,72,1024]{2,1,0:T(8,128)(2,1)S(1)}, u32[]{:S(2)}, u32[]{:S(2)}) async-start(bf16[4,72,1024]{2,1,0:T(8,128)(2,1)} %bitcast.27), calls=%async_computation.2 | async-start | bytes 1179648 | tf_op jit(solution)/shard_map/all_to_all | solution.py:232
  372.6 36.5 %copy-start.63 = (f32[256]{0:T(256)S(1)}, f32[256]{0:T(256)}, u32[]{:S(2)}) copy-start(f32[256]{0:T(256)} %copy-done.62) | copy-start | bytes 3076
  372.6 36.6 %copy-start.65 = (f32[256]{0:T(256)S(1)}, f32[256]{0:T(256)}, u32[]{:S(2)}) copy-start(f32[256]{0:T(256)} %copy-done.64) | copy-start | bytes 3076
  387.0 19.8 %all-to-all-start.3 = ((bf16[4,72,1024]{2,1,0:T(8,128)(2,1)}), bf16[4,72,1024]{2,1,0:T(8,128)(2,1)}, u32[]{:S(2)}, u32[]{:S(2)}) async-start(bf16[4,72,1024]{2,1,0:T(8,128)(2,1)} %bitcast.31), calls=%async_computation.3 | async-start | bytes 1179648 | tf_op jit(solution)/shard_map/all_to_all | solution.py:232
  412.9 12.7 %copy-start.32 = (bf16[256,1024]{1,0:T(8,128)(2,1)}, bf16[256,1024]{1,0:T(8,128)(2,1)S(1)}, u32[]{:S(2)}) copy-start(bf16[256,1024]{1,0:T(8,128)(2,1)S(1)} %fusion.83) | copy-start | bytes 1572868
  414.5 11.8 %all-to-all-start.4 = ((bf16[256,4,256]{2,0,1:T(8,128)(2,1)}), bf16[256,4,256]{2,0,1:T(8,128)(2,1)}, u32[]{:S(2)}, u32[]{:S(2)}) async-start(bf16[256,4,256]{2,0,1:T(8,128)(2,1)} %bitcast.189), calls=%async_computation.4 | async-start | bytes 1048576 | tf_op jit(solution)/shard_map/all_to_all | solution.py:53
  418.6 106.7 %reduce-scatter.20.cloned.1.call-start = ((), (), s32[]{:S(2)}) async-start(), calls=%async_computation.22 | async-start | bytes 5242880 | tf_op jit(solution)/shard_map/reduce_scatter | solution.py:277
  425.6 107.6 %reduce-scatter.8.cloned.1.call-start = ((), (), s32[]{:S(2)}) async-start(), calls=%async_computation.15 | async-start | bytes 2621440 | tf_op jit(solution)/shard_map/reduce_scatter | solution.py:319
  498.5 90.8 %reduce-scatter.14.cloned.1.call-start = ((), (), s32[]{:S(2)}) async-start(), calls=%async_computation.19 | async-start | bytes 5242880 | tf_op jit(solution)/shard_map/reduce_scatter | solution.py:277
  505.4 136.0 %reduce-scatter.12.cloned.1.call-start = ((), (), s32[]{:S(2)}) async-start(), calls=%async_computation.17 | async-start | bytes 4718592 | tf_op jit(solution)/shard_map/reduce_scatter | solution.py:333
  509.2 186.3 %reduce-scatter.16.cloned.1.call-start = ((), (), s32[]{:S(2)}) async-start(), calls=%async_computation.20 | async-start | bytes 5242880 | tf_op jit(solution)/shard_map/reduce_scatter | solution.py:277
  516.4 221.7 %reduce-scatter.10.cloned.1.call-start = ((), (), s32[]{:S(2)}) async-start(), calls=%async_computation.16 | async-start | bytes 3538944 | tf_op jit(solution)/shard_map/reduce_scatter | solution.py:325
  521.8 11.4 %copy-start.7 = (bf16[1,256,1024]{2,1,0:T(8,128)(2,1)S(1)}, bf16[1,256,1024]{2,1,0:T(8,128)(2,1)}, u32[]{:S(2)}) copy-start(bf16[1,256,1024]{2,1,0:T(8,128)(2,1)} %param.17) | copy-start | bytes 1572868
  521.8 11.4 %copy-start.41 = (f32[8,1,128]{2,1,0:T(1,128)S(1)}, f32[8,1,128]{2,1,0:T(1,128)}, u32[]{:S(2)}) copy-start(f32[8,1,128]{2,1,0:T(1,128)} %copy-done.40) | copy-start | bytes 12292
  521.8 11.4 %copy-start.47 = (f32[256]{0:T(256)S(1)}, f32[256]{0:T(256)}, u32[]{:S(2)}) copy-start(f32[256]{0:T(256)} %copy-done.46) | copy-start | bytes 3076
  521.9 12.7 %copy-start.61 = (f32[256]{0:T(256)S(1)}, f32[256]{0:T(256)}, u32[]{:S(2)}) copy-start(f32[256]{0:T(256)} %copy-done.60) | copy-start | bytes 3076
  521.9 12.7 %copy-start.53 = (f32[256]{0:T(256)S(1)}, f32[256]{0:T(256)}, u32[]{:S(2)}) copy-start(f32[256]{0:T(256)} %copy-done.52) | copy-start | bytes 3076
  521.9 55.4 %copy-start.12 = (f32[256,1024]{1,0:T(8,128)S(1)}, f32[256,1024]{1,0:T(8,128)}, u32[]{:S(2)}) copy-start(f32[256,1024]{1,0:T(8,128)} %copy-done.11) | copy-start | bytes 3145732
  521.9 55.4 %copy-start.15 = (bf16[1,256,1024]{2,1,0:T(8,128)(2,1)S(1)}, bf16[1,256,1024]{2,1,0:T(8,128)(2,1)}, u32[]{:S(2)}) copy-start(bf16[1,256,1024]{2,1,0:T(8,128)(2,1)} %param.29) | copy-start | bytes 1572868
  521.9 263.0 %all-reduce.2.cloned.1.call-start = ((), (), s32[]{:S(2)}) async-start(), calls=%async_computation.18 | async-start | bytes 524288 | tf_op jit(solution)/shard_map/psum | solution.py:334
  (41 other events, 148.7 us)
Sparse Core Ops, SparseCore 0:
  10.2 29.7 all-gather.16
  42.4 33.9 all-gather.14
  78.0 29.1 all-gather.18
  108.9 52.0 all-gather.20
  162.7 52.5 all-gather.22
  217.0 52.5 all-gather.24
  271.4 52.5 all-gather.26
  342.0 52.7 reduce-scatter.17
  425.7 52.0 reduce-scatter.19
  498.6 34.5 reduce-scatter.7
  536.2 53.0 reduce-scatter.13
  591.4 50.0 reduce-scatter.11
  644.4 51.0 reduce-scatter.15
  697.7 40.3 reduce-scatter.9
  741.5 43.4 all-reduce.1
where the time goes:
time: 803 us; the launch traced here: 794 us
  waiting for transfers between devices  384 us (48%)
  matrix products  172 us (21%)
  blocking collectives  109 us (14%)
  other arithmetic  49.1 us (6%)
  local copies, waits for them, and re-layouts  37.7 us (5%)
  starting transfers between devices  18 us (2%)
  between operations  15.5 us (2%)
  loops' own time  8.29 us (1%)
    all_gather x4, waiting for transfers between devices, local(): lax.all_gather(part[0], 'seq', axis=0, tiled=True)  118 us
    reduce_scatter x4, waiting for transfers between devices, weight_grad(): lax.psum_scatter(dot_rows(left, right).astype(jnp.bfloat16), 'seq', scatt...  61.8 us
    dot_general x7, matrix products, dot_last(): lax.dot_general(left_mat, right_mat, (((1,), (1,)), ((), ())), preferred_...  54.8 us
    reduce_scatter x1, waiting for transfers between devices, local(): lax.psum_scatter(grad_out_full, 'wshard', scatter_dimension=0, tiled=True)  49.5 us
    psum x1, blocking collectives, local(): small = lax.psum(small, ('seq', 'wshard'))  39.9 us
    reduce_scatter x1, waiting for transfers between devices, local(): lax.psum_scatter(grad_qkv_heads, 'wshard', scatter_dimension=0, tiled=True)  39.8 us
    dot_general x8, matrix products, dot_rows(): lax.dot_general(left_mat, right_mat, (((0,), (0,)), ((), ())), preferred_...  38.8 us
    all_gather x1, waiting for transfers between devices, local(): normed_all = lax.all_gather(normed_one, 'seq', axis=0, tiled=True)  36.4 us
  transfers between devices with their start and end apart: 24, of which 16 were waited for; matrix products, arithmetic and copies ran while one was open for 29% of the time, Pallas kernels for 0%

commit v1 on v0

--- a/solution.py
+++ b/solution.py
@@ -6,6 +6,22 @@
 HEAD = 64
 EPSILON = 1e-05
 NEG_FILL = -1e30
+
+
+def gather_around(x, axis, dim):
+    ways, here, step = (lax.axis_size(axis), lax.axis_index(axis), x.shape[dim])
+    lengths = [n * ways if d == dim else n for d, n in enumerate(x.shape)]
+    full = lax.dynamic_update_slice_in_dim(jnp.zeros(lengths, x.dtype), x, here * step, axis=dim)
+    going_up = going_down = x
+    for far in range(1, ways // 2 + 1):
+        going_up = lax.ppermute(going_up, axis, [(d, (d + 1) % ways) for d in range(ways)])
+        full = lax.dynamic_update_slice_in_dim(full, going_up, (here - far) % ways * step, axis=dim)
+        if 2 * far < ways:
+            going_down = lax.ppermute(going_down, axis, [(d, (d - 1) % ways) for d in range(ways)])
+            full = lax.dynamic_update_slice_in_dim(
+                full, going_down, (here + far) % ways * step, axis=dim
+            )
+    return full
 
 
 def as_sent(shard):
@@ -193,7 +209,7 @@
     gain_second = full_gain_two.astype(jnp.float32)
     tokens_in = inputs[0].astype(jnp.float32)
     normed_one = norm_rows(tokens_in, gain_first).astype(jnp.bfloat16)
-    normed_all = lax.all_gather(normed_one, "seq", axis=0, tiled=True)
+    normed_all = gather_around(normed_one, "seq", 0)
     full_out = lax.all_gather(out_weight, "wshard", axis=0, tiled=True)
     up_a, down_a, up_b, down_b = (
         lax.all_gather(part[0], "seq", axis=0, tiled=True)

time: 803 us -> 767 us (0.955)
  waiting for transfers between devices: 384 us -> 349 us
    all_gather x1 -> x0, waiting for transfers between devices: 36.4 us -> none  [local(): normed_all = lax.all_gather(normed_one, 'seq', axis=0, tiled=True)]
    ppermute x0 -> x3, waiting for transfers between devices: none -> 31.8 us  [the longest x2 22.3 us: gather_around(): lax.ppermute(going_up, axis, [(d, (d + 1) % ways) for d in range(ways)])]
    all_gather x4, waiting for transfers between devices: 118 us -> 92.7 us  [local(): lax.all_gather(part[0], 'seq', axis=0, tiled=True)]
    all_gather x1, waiting for transfers between devices: 8.58 us -> 0.02 us  [local(): lax.all_gather(qkv_own.reshape(-1, 3 * head_width), 'wshard', axis=0, til...]
  transfers between devices with their start and end apart: 24 -> 26, of which waited for: 16 -> 18; matrix products, arithmetic and copies ran while one was open for 29% -> 30% of each run, Pallas kernels for 0% -> 0%
where the time goes in v1:
time: 767 us; the launch traced here: 758 us
  waiting for transfers between devices  349 us (46%)
  matrix products  170 us (22%)
  blocking collectives  104 us (14%)
  local copies, waits for them, and re-layouts  45 us (6%)
  other arithmetic  44.2 us (6%)
  starting transfers between devices  21.4 us (3%)
  between operations  15.5 us (2%)
  loops' own time  8.27 us (1%)
    all_gather x4, waiting for transfers between devices, local(): lax.all_gather(part[0], 'seq', axis=0, tiled=True)  92.7 us
    reduce_scatter x4, waiting for transfers between devices, weight_grad(): lax.psum_scatter(dot_rows(left, right).astype(jnp.bfloat16), 'seq', scatt...  61.5 us
    dot_general x7, matrix products, dot_last(): lax.dot_general(left_mat, right_mat, (((1,), (1,)), ((), ())), preferred_...  54.8 us
    reduce_scatter x1, waiting for transfers between devices, local(): lax.psum_scatter(grad_out_full, 'wshard', scatter_dimension=0, tiled=True)  49.6 us
    reduce_scatter x1, waiting for transfers between devices, local(): lax.psum_scatter(grad_qkv_heads, 'wshard', scatter_dimension=0, tiled=True)  39.9 us
    psum x1, blocking collectives, local(): small = lax.psum(small, ('seq', 'wshard'))  39.9 us
    dot_general x8, matrix products, dot_rows(): lax.dot_general(left_mat, right_mat, (((0,), (0,)), ((), ())), preferred_...  38.1 us
    psum x1, waiting for transfers between devices, local(): lax.psum(out_part.astype(jnp.bfloat16), 'seq').astype(jnp.float32)  30.8 us
  transfers between devices with their start and end apart: 26, of which 18 were waited for; matrix products, arithmetic and copies ran while one was open for 30% of the time, Pallas kernels for 0%

profile of v1, /device:TPU:0, one launch (start us, length us, event | category | flops | bytes accessed | tf_op | source)
XLA Modules:
  0.0 757.9 jit_solution(15004464381762327257)
XLA Ops:
  11.7 13.6 %all-gather.5 = bf16[8,1,128]{2,1,0:T(2,128)(2,1)S(1)} all-gather(bf16[1,1,128]{2,1,0:T(2,128)(2,1)S(1)} %bitcast.285), channel_id=1, replica_groups=mesh['seq'=4,'wshard'=8] {'wshard'}, dimensions={0}, use_global_device_ids=true | all-gather | bytes 2304 | tf_op jit(solution)/shard_map/all_gather | solution.py:206
  29.8 12.9 %collective-permute-done = bf16[256,1024]{1,0:T(8,128)(2,1)} collective-permute-done((bf16[256,1024]{1,0:T(8,128)(2,1)S(1)}, bf16[256,1024]{1,0:T(8,128)(2,1)}, u32[]{:S(2)}, u32[]{:S(2)}) %collective-permute-start) | collective-permute-done | bytes 524320 | tf_op jit(solution)/shard_map/ppermute | solution.py:17
  44.6 9.4 %collective-permute-done.1 = bf16[256,1024]{1,0:T(8,128)(2,1)} collective-permute-done((bf16[256,1024]{1,0:T(8,128)(2,1)S(1)}, bf16[256,1024]{1,0:T(8,128)(2,1)}, u32[]{:S(2)}, u32[]{:S(2)}) %collective-permute-start.1) | collective-permute-done | bytes 524320 | tf_op jit(solution)/shard_map/ppermute | solution.py:20
  55.1 9.5 %collective-permute-done.2 = bf16[256,1024]{1,0:T(8,128)(2,1)} collective-permute-done((bf16[256,1024]{1,0:T(8,128)(2,1)}, bf16[256,1024]{1,0:T(8,128)(2,1)}, u32[]{:S(2)}, u32[]{:S(2)}) %collective-permute-start.2) | collective-permute-done | bytes 524320 | tf_op jit(solution)/shard_map/ppermute | solution.py:17
  67.0 3.2 convolution_convert_fusion.6
  71.9 24.4 %while.27 = (s32[]{:T(128)}, bf16[2,512,256]{2,1,0:T(8,128)(2,1)}, f32[2,4,512]{2,1,0:T(4,128)S(1)}, s32[1,1024]{1,0:T(1,128)S(1)}, s32[2]{0:T(128)S(1)}, /*inde...) while((s32[]{:T(128)}, bf16[2,512,256]{2,1,0:T(8,128)(2,1)}, ...), condition=%wide.region_5.6_spmd, body=%wide.region_2.5_spmd.sunk | while | flops 562690048 | bytes 30485168 | solution.py:113
  77.8 2.4 fusion.189
  80.2 3.1 fusion.190
  90.0 2.4 fusion.189
  92.4 3.1 fusion.190
  96.4 3.5 all-to-all-start
  100.0 8.4 %all-gather.6 = bf16[8,1,128]{2,1,0:T(2,128)(2,1)S(1)} all-gather(bf16[1,1,128]{2,1,0:T(2,128)(2,1)S(1)} %bitcast.286), channel_id=1, replica_groups=mesh['seq'=4,'wshard'=8] {'wshard'}, dimensions={0}, use_global_device_ids=true | all-gather | bytes 2304 | tf_op jit(solution)/shard_map/all_gather | solution.py:207
  108.7 5.7 all-to-all-done
  114.6 2.6 fusion.123
  119.4 30.1 %all_to_all.53 = bf16[4,72,2048]{2,1,0:T(8,128)(2,1)S(1)} all-to-all(bf16[4,72,2048]{2,1,0:T(8,128)(2,1)S(1)} %bitcast.261), channel_id=1, replica_groups={{0,2,4,6},{1,3,5,7},{8,10,12,14},{9,11,13,15},{16,18,20,22},{17,19,21,2..., dimensions={0} | all-to-all | bytes 2359296 | tf_op jit(solution)/shard_map/all_to_all | solution.py:248
  152.6 16.8 %multiply_convert_fusion.2 = (bf16[576,2048]{1,0:T(8,128)(2,1)}, f32[576,2048]{1,0:T(8,128)}, f32[576,2048]{1,0:T(8,128)}) fusion(bf16[1,2048,1024]{2,1,0:T(8,128)(2,1)} %all-gather.18.cloned.1.call-done, bf16[288,1024]{1,0:T(8,128)(2,1)S(1)} %get-tuple-element.271, bf16[288,1024]{1,0:T(8,128)(2,1)S(1)} %get-tuple-element.269), kind=kOutput, calls=%fused_computation.52 | convolution fusion | flops 2494955520 | bytes 17170432 | tf_op jit(solution)/shard_map/dot_general | solution.py:61
  169.4 11.7 %all-gather.20.cloned.1.call-done = bf16[1,2048,1024]{2,1,0:T(8,128)(2,1)} async-done(((bf16[1,512,1024]{2,1,0:T(8,128)(2,1)}), bf16[1,2048,1024]{2,1,0:T(8,128)(2,1)}) %all-gather.20.cloned.1.call-update) | async-done | bytes 4194320 | tf_op jit(solution)/shard_map/all_gather | solution.py:215
  181.1 5.1 fusion.43
  186.2 4.5 collective-permute-done.4
  191.8 43.5 %all-gather.22.cloned.1.call-done = bf16[1,2048,1024]{2,1,0:T(8,128)(2,1)} async-done(((bf16[1,512,1024]{2,1,0:T(8,128)(2,1)}), bf16[1,2048,1024]{2,1,0:T(8,128)(2,1)}) %all-gather.22.cloned.1.call-update) | async-done | bytes 4194320 | tf_op jit(solution)/shard_map/all_gather | solution.py:215
  235.4 16.8 %multiply_convert_fusion.1 = (bf16[576,2048]{1,0:T(8,128)(2,1)}, f32[576,2048]{1,0:T(8,128)}, f32[576,2048]{1,0:T(8,128)}) fusion(bf16[576,1024]{1,0:T(8,128)(2,1)S(1)} %fusion.54, bf16[1,2048,1024]{2,1,0:T(8,128)(2,1)} %all-gather.22.cloned.1.call-done), kind=kOutput, calls=%fused_computation.39 | convolution fusion | flops 2492596224 | bytes 17170432 | tf_op jit(solution)/shard_map/dot_general | solution.py:61
  252.2 37.5 %all-gather.24.cloned.1.call-done = bf16[1,2048,1024]{2,1,0:T(8,128)(2,1)} async-done(((bf16[1,512,1024]{2,1,0:T(8,128)(2,1)}), bf16[1,2048,1024]{2,1,0:T(8,128)(2,1)}) %all-gather.24.cloned.1.call-update) | async-done | bytes 4194320 | tf_op jit(solution)/shard_map/all_gather | solution.py:215
  289.7 8.6 %add_convert_fusion.1 = bf16[576,2048]{1,0:T(8,128)(2,1)S(1)} fusion(f32[576,2048]{1,0:T(8,128)} %get-tuple-element.250, f32[576,2048]{1,0:T(8,128)} %get-tuple-element.278, bf16[1,2048,1024]{2,1,0:T(8,128)(2,1)} %all-gather.24.cloned.1.call-done, bf16[288,1024]{1,0:T(8,128)(2,1)S(1)} %get-tuple-element.270, bf16[288,1024]{1,0:T(8,128)(2,1)S(1)} %copy-done.27), kind=kOutput, calls=%fused_computation.38 | convolution fusion | flops 2434793472 | bytes 17170432 | tf_op jit(solution)/shard_map/dot_general | solution.py:61
  298.3 4.1 fusion.37
  302.5 5.0 convolution_convert_fusion.1
  307.5 5.3 fusion.35
  313.5 2.4 fusion.117
  315.9 2.4 fusion.56
  318.8 6.8 add_convert_fusion
  325.6 2.6 fusion.45
  330.6 4.5 all-to-all-start.2
  335.2 3.0 fusion.65
  338.2 13.4 %all-to-all-done.2 = bf16[4,72,1024]{2,1,0:T(8,128)(2,1)S(1)} async-done(((bf16[4,72,1024]{2,1,0:T(8,128)(2,1)}), bf16[4,72,1024]{2,1,0:T(8,128)(2,1)S(1)}, u32[]{:S(2)}, u32[]{:S(2)}) %all-to-all-start.2) | async-done | bytes 589856 | tf_op jit(solution)/shard_map/all_to_all | solution.py:248
  352.4 4.2 all-to-all-start.3
  356.6 2.5 fusion.75
  360.5 11.7 %all-to-all-done.3 = bf16[4,72,1024]{2,1,0:T(8,128)(2,1)} async-done(((bf16[4,72,1024]{2,1,0:T(8,128)(2,1)}), bf16[4,72,1024]{2,1,0:T(8,128)(2,1)}, u32[]{:S(2)}, u32[]{:S(2)}) %all-to-all-start.3) | async-done | bytes 589856 | tf_op jit(solution)/shard_map/all_to_all | solution.py:248
  378.6 4.1 all-to-all-start.4
  382.8 6.9 convolution_convert_fusion
  391.3 64.6 %while.28 = (s32[]{:T(128)}, f32[1024,4,64]{0,2,1:T(8,128)S(1)}, f32[1024,4,64]{0,2,1:T(8,128)}, bf16[2,512,256]{2,1,0:T(8,128)(2,1)}, s32[2]{0:T(128)S(1)}, /*i...) while((s32[]{:T(128)}, f32[1024,4,64]{0,2,1:T(8,128)S(1)}, ...), condition=%wide.region_15.16_spmd.clone, body=%wide.region_13.15_spmd.clone.sunk | while | flops 1375729664 | bytes 118819648 | solution.py:169
  395.2 4.7 fusion.201
  401.5 6.1 multiply_reduce_fusion.5
  414.6 3.2 fusion.202
  417.8 6.0 fusion.203
  427.5 4.7 fusion.201
  433.8 5.8 multiply_reduce_fusion.5
  446.6 3.1 fusion.202
  449.7 6.2 fusion.203
  458.0 4.7 convolution_convert_fusion.5
  462.8 6.8 convolution_convert_fusion.3
  470.8 2.7 fusion.125
  474.8 7.1 convolution_convert_fusion.2
  483.6 4.8 fusion.84
  489.2 2.9 bitcast_convert_fusion.1
  492.1 2.8 bitcast_convert_fusion
  494.9 2.5 reduce-scatter.8.cloned.1.call-done
  500.5 39.9 %psum.15 = f32[6,1024]{1,0:T(8,128)S(1)} all-reduce(f32[6,1024]{1,0:T(8,128)S(1)} %pad_maximum_fusion.9), channel_id=1, replica_groups=mesh['seq'=4,'wshard'=8] {'seq','wshard'}, use_global_device_ids=true, to_apply=%region_24.25 | all-reduce | flops 6144 | bytes 49152 | tf_op jit(solution)/shard_map/psum | solution.py:352
  543.9 9.4 %reduce-scatter.14.cloned.1.call-done = bf16[512,1024]{1,0:T(8,128)(2,1)} async-done(((bf16[2048,1024]{1,0:T(8,128)(2,1)}), bf16[512,1024]{1,0:T(8,128)(2,1)}) %reduce-scatter.14.cloned.1.call-update) | async-done | bytes 1048592 | tf_op jit(solution)/shard_map/reduce_scatter | solution.py:293
  553.3 2.8 bitcast_convert_fusion.3
  556.1 49.6 %reduce-scatter.12.cloned.1.call-done = f32[128,1024]{1,0:T(8,128)} async-done(((f32[1024,1024]{1,0:T(8,128)}), f32[128,1024]{1,0:T(8,128)}) %reduce-scatter.12.cloned.1.call-update) | async-done | bytes 524304 | tf_op jit(solution)/shard_map/reduce_scatter | solution.py:349
  607.5 52.1 %reduce-scatter.16.cloned.1.call-done = bf16[512,1024]{1,0:T(8,128)(2,1)} async-done(((bf16[2048,1024]{1,0:T(8,128)(2,1)}), bf16[512,1024]{1,0:T(8,128)(2,1)}) %reduce-scatter.16.cloned.1.call-update) | async-done | bytes 1048592 | tf_op jit(solution)/shard_map/reduce_scatter | solution.py:293
  659.6 2.8 bitcast_convert_fusion.2
  662.4 39.9 %reduce-scatter.10.cloned.1.call-done = f32[128,768]{1,0:T(8,128)} async-done(((f32[1024,768]{1,0:T(8,128)}), f32[128,768]{1,0:T(8,128)}) %reduce-scatter.10.cloned.1.call-update) | async-done | bytes 393232 | tf_op jit(solution)/shard_map/reduce_scatter | solution.py:341
  703.4 12.4 %all-gather.4 = bf16[512,768]{1,0:T(8,128)(2,1)S(1)} all-gather(bf16[128,768]{1,0:T(8,128)(2,1)S(1)} %convert_element_type.235), channel_id=6, replica_groups=mesh['seq'=4,'wshard'=8] {'seq'}, dimensions={0}, use_global_device_ids=true | all-gather | bytes 983040 | tf_op jit(solution)/shard_map/all_gather | solution.py:342
  718.4 30.8 %all-reduce.2.cloned.1.call-done = bf16[128,1024]{1,0:T(8,128)(2,1)} async-done(((bf16[128,1024]{1,0:T(8,128)(2,1)}), bf16[128,1024]{1,0:T(8,128)(2,1)}) %all-reduce.2.cloned.1.call-update) | async-done | bytes 262160 | tf_op jit(solution)/shard_map/psum | solution.py:350
  (324 shorter events, 86.8 us)
Async XLA Ops:
  7.2 111.2 %copy-start = (bf16[4,1024]{1,0:T(4,128)(2,1)S(1)}, bf16[4,1024]{1,0:T(4,128)(2,1)}, u32[]{:S(2)}) copy-start(bf16[4,1024]{1,0:T(4,128)(2,1)} %param.24) | copy-start | bytes 24580
  7.2 18.0 %copy-start.6 = (bf16[1,256,1024]{2,1,0:T(8,128)(2,1)S(1)}, bf16[1,256,1024]{2,1,0:T(8,128)(2,1)}, u32[]{:S(2)}) copy-start(bf16[1,256,1024]{2,1,0:T(8,128)(2,1)} %param.17) | copy-start | bytes 1572868
  7.2 58.5 %all-gather.14.cloned.1.call-start = ((), (), s32[]{:S(2)}) async-start(), calls=%async_computation.12 | async-start | bytes 1769472 | tf_op jit(solution)/shard_map/all_gather | solution.py:205
  9.6 105.1 %all-gather.16.cloned.1.call-start = ((), (), s32[]{:S(2)}) async-start(), calls=%async_computation.13 | async-start | bytes 2359296 | tf_op jit(solution)/shard_map/all_gather | solution.py:213
  10.3 142.3 %all-gather.18.cloned.1.call-start = ((), (), s32[]{:S(2)}) async-start(), calls=%async_computation.22 | async-start | bytes 5242880 | tf_op jit(solution)/shard_map/all_gather | solution.py:215
  11.0 170.0 %all-gather.20.cloned.1.call-start = ((), (), s32[]{:S(2)}) async-start(), calls=%async_computation.23 | async-start | bytes 5242880 | tf_op jit(solution)/shard_map/all_gather | solution.py:215
  11.6 223.8 %all-gather.22.cloned.1.call-start = ((), (), s32[]{:S(2)}) async-start(), calls=%async_computation.24 | async-start | bytes 5242880 | tf_op jit(solution)/shard_map/all_gather | solution.py:215
  25.2 17.5 %copy-start.43 = (f32[8,1,128]{2,1,0:T(1,128)}, f32[8,1,128]{2,1,0:T(1,128)S(1)}, u32[]{:S(2)}) copy-start(f32[8,1,128]{2,1,0:T(1,128)S(1)} %convert_element_type.252) | copy-start | bytes 12292
  25.4 17.3 %copy-start.49 = (f32[256]{0:T(256)}, f32[256]{0:T(256)S(1)}, u32[]{:S(2)}) copy-start(f32[256]{0:T(256)S(1)} %broadcast_multiply_fusion.1) | copy-start | bytes 3076
  26.3 16.4 %copy-start.55 = (f32[256]{0:T(256)}, f32[256]{0:T(256)S(1)}, u32[]{:S(2)}) copy-start(f32[256]{0:T(256)S(1)} %fusion.102) | copy-start | bytes 3076
  26.8 15.9 %collective-permute-start = (bf16[256,1024]{1,0:T(8,128)(2,1)S(1)}, bf16[256,1024]{1,0:T(8,128)(2,1)}, u32[]{:S(2)}, u32[]{:S(2)}) collective-permute-start(bf16[256,1024]{1,0:T(8,128)(2,1)S(1)} %get-tuple-element.256), channel_id=1, source_target_pairs={{0,8},{8,16},{16,24},{24,0},{1,9},{9,17},{17,25},{25,1},{2,10},{10... | collective-permute-start | bytes 1572872 | tf_op jit(solution)/shard_map/ppermute | solution.py:17
  28.4 25.6 %collective-permute-start.1 = (bf16[256,1024]{1,0:T(8,128)(2,1)S(1)}, bf16[256,1024]{1,0:T(8,128)(2,1)}, u32[]{:S(2)}, u32[]{:S(2)}) collective-permute-start(bf16[256,1024]{1,0:T(8,128)(2,1)S(1)} %get-tuple-element.256), channel_id=1, source_target_pairs={{0,24},{8,0},{16,8},{24,16},{1,25},{9,1},{17,9},{25,17},{2,26},{10... | collective-permute-start | bytes 1572872 | tf_op jit(solution)/shard_map/ppermute | solution.py:20
  42.7 21.8 %collective-permute-start.2 = (bf16[256,1024]{1,0:T(8,128)(2,1)}, bf16[256,1024]{1,0:T(8,128)(2,1)}, u32[]{:S(2)}, u32[]{:S(2)}) collective-permute-start(bf16[256,1024]{1,0:T(8,128)(2,1)} %collective-permute-done), channel_id=1, source_target_pairs={{0,8},{8,16},{16,24},{24,0},{1,9},{9,17},{17,25},{25,1},{2,10},{10... | collective-permute-start | bytes 1572872 | tf_op jit(solution)/shard_map/ppermute | solution.py:17
  71.9 28.0 %copy-start.72 = (bf16[128]{0:T(256)(128)(2,1)S(1)}, bf16[128]{0:T(256)(128)(2,1)}, u32[]{:S(2)}) copy-start(bf16[128]{0:T(256)(128)(2,1)} %param.23) | copy-start | bytes 772
  71.9 36.5 %copy-start.53 = (s32[1,256,1]{1,2,0:T(1,128)S(1)}, s32[1,256,1]{1,2,0:T(1,128)}, u32[]{:S(2)}) copy-start(s32[1,256,1]{1,2,0:T(1,128)} %param.18) | copy-start | bytes 3076
  96.4 12.1 %copy-start.76 = (s32[2]{0:T(128)}, s32[2]{0:T(128)S(1)}, u32[]{:S(2)}) copy-start(s32[2]{0:T(128)S(1)} %get-tuple-element.586) | copy-start | bytes 28
  96.4 22.0 %copy-start.2 = (bf16[1024,4,64]{0,2,1:T(8,128)(2,1)}, bf16[1024,4,64]{0,2,1:T(8,128)(2,1)S(1)}, u32[]{:S(2)}) copy-start(bf16[1024,4,64]{0,2,1:T(8,128)(2,1)S(1)} %get-tuple-element.515) | copy-start | bytes 1572868
  96.4 22.0 %copy-start.8 = (bf16[1024,4,64]{0,2,1:T(8,128)(2,1)}, bf16[1024,4,64]{0,2,1:T(8,128)(2,1)S(1)}, u32[]{:S(2)}) copy-start(bf16[1024,4,64]{0,2,1:T(8,128)(2,1)S(1)} %get-tuple-element.518) | copy-start | bytes 1572868
  96.4 22.0 %copy-start.45 = (f32[2,4,512]{2,1,0:T(4,128)}, f32[2,4,512]{2,1,0:T(4,128)S(1)}, u32[]{:S(2)}) copy-start(f32[2,4,512]{2,1,0:T(4,128)S(1)} %get-tuple-element.124) | copy-start | bytes 49156
  96.4 18.0 %all-to-all-start = ((bf16[4,256,256]{2,1,0:T(8,128)(2,1)}), bf16[4,256,256]{2,1,0:T(8,128)(2,1)S(1)}, u32[]{:S(2)}, u32[]{:S(2)}) async-start(bf16[4,256,256]{2,1,0:T(8,128)(2,1)} %bitcast.14), calls=%async_computation | async-start | bytes 1048576 | tf_op jit(solution)/shard_map/all_to_all | solution.py:77
  99.9 189.7 %all-gather.24.cloned.1.call-start = ((), (), s32[]{:S(2)}) async-start(), calls=%async_computation.25 | async-start | bytes 5242880 | tf_op jit(solution)/shard_map/all_gather | solution.py:215
  108.4 10.3 %copy-start.47 = (f32[8,1,128]{2,1,0:T(1,128)}, f32[8,1,128]{2,1,0:T(1,128)S(1)}, u32[]{:S(2)}) copy-start(f32[8,1,128]{2,1,0:T(1,128)S(1)} %convert_element_type.253) | copy-start | bytes 12292
  108.7 10.3 %copy-start.59 = (s32[256]{0:T(256)}, s32[256]{0:T(256)S(1)}, u32[]{:S(2)}) copy-start(s32[256]{0:T(256)S(1)} %multiply_add_fusion) | copy-start | bytes 3076
  117.2 32.3 %copy-start.51 = (f32[256]{0:T(256)}, f32[256]{0:T(256)S(1)}, u32[]{:S(2)}) copy-start(f32[256]{0:T(256)S(1)} %broadcast_multiply_fusion) | copy-start | bytes 3076
  117.5 32.1 %copy-start.57 = (f32[256]{0:T(256)}, f32[256]{0:T(256)S(1)}, u32[]{:S(2)}) copy-start(f32[256]{0:T(256)S(1)} %fusion.103) | copy-start | bytes 3076
  118.7 32.1 %copy-start.61 = (f32[256]{0:T(256)}, f32[256]{0:T(256)S(1)}, u32[]{:S(2)}) copy-start(f32[256]{0:T(256)S(1)} %fusion.68) | copy-start | bytes 3076
  118.7 30.9 %copy-start.67 = (f32[256]{0:T(256)}, f32[256]{0:T(256)S(1)}, u32[]{:S(2)}) copy-start(f32[256]{0:T(256)S(1)} %get-tuple-element.253) | copy-start | bytes 3076
  118.7 32.1 %copy-start.69 = (pred[256]{0:T(512)(128)(4,1)}, pred[256]{0:T(512)(128)(4,1)S(1)}, u32[]{:S(2)}) copy-start(pred[256]{0:T(512)(128)(4,1)S(1)} %get-tuple-element.254) | copy-start | bytes 772
  149.6 2.8 collective-permute-start.3
  149.6 339.5 %reduce-scatter.18.cloned.1.call-start = ((), (), s32[]{:S(2)}) async-start(), calls=%async_computation.20 | async-start | bytes 5242880 | tf_op jit(solution)/shard_map/reduce_scatter | solution.py:293
  150.8 40.3 %copy-start.23 = (bf16[288,1024]{1,0:T(8,128)(2,1)}, bf16[288,1024]{1,0:T(8,128)(2,1)S(1)}, u32[]{:S(2)}) copy-start(bf16[288,1024]{1,0:T(8,128)(2,1)S(1)} %get-tuple-element.269) | copy-start | bytes 1769476
  152.5 38.5 %copy-start.25 = (bf16[288,1024]{1,0:T(8,128)(2,1)}, bf16[288,1024]{1,0:T(8,128)(2,1)S(1)}, u32[]{:S(2)}) copy-start(bf16[288,1024]{1,0:T(8,128)(2,1)S(1)} %get-tuple-element.271) | copy-start | bytes 1769476
  152.5 163.4 %copy-start.28 = (bf16[288,1024]{1,0:T(8,128)(2,1)}, bf16[288,1024]{1,0:T(8,128)(2,1)S(1)}, u32[]{:S(2)}) copy-start(bf16[288,1024]{1,0:T(8,128)(2,1)S(1)} %get-tuple-element.270) | copy-start | bytes 1769476
  186.2 4.6 collective-permute-start.4
  191.8 97.8 %copy-start.27 = (bf16[288,1024]{1,0:T(8,128)(2,1)S(1)}, bf16[288,1024]{1,0:T(8,128)(2,1)}, u32[]{:S(2)}) copy-start(bf16[288,1024]{1,0:T(8,128)(2,1)} %get-tuple-element.268) | copy-start | bytes 1769476
  302.5 11.0 %collective-permute-start.6 = (f32[576,1024]{1,0:T(8,128)}, f32[576,1024]{1,0:T(8,128)}, u32[]{:S(2)}, u32[]{:S(2)}) collective-permute-start(f32[576,1024]{1,0:T(8,128)} %fusion.37), channel_id=1, source_target_pairs={{0,1},{1,0},{2,3},{3,2},{4,5},{5,4},{6,7},{7,6},{8,9},{9,8},{10,11... | collective-permute-start | bytes 7077896 | tf_op jit(solution)/shard_map/ppermute | solution.py:36
  312.9 16.6 %collective-permute-start.5 = (f32[288,1024]{1,0:T(8,128)S(1)}, f32[288,1024]{1,0:T(8,128)S(1)}, u32[]{:S(2)}, u32[]{:S(2)}) collective-permute-start(f32[288,1024]{1,0:T(8,128)S(1)} %slice.89), channel_id=1, source_target_pairs={{0,1},{1,0},{2,3},{3,2},{4,5},{5,4},{6,7},{7,6},{8,9},{9,8},{10,11... | collective-permute-start | bytes 3538952 | tf_op jit(solution)/shard_map/ppermute | solution.py:36
  329.4 27.1 %copy-start.14 = (bf16[1,256,1024]{2,1,0:T(8,128)(2,1)S(1)}, bf16[1,256,1024]{2,1,0:T(8,128)(2,1)}, u32[]{:S(2)}) copy-start(bf16[1,256,1024]{2,1,0:T(8,128)(2,1)} %param.29) | copy-start | bytes 1572868
  329.4 27.2 %copy-start.60 = (s32[256]{0:T(256)S(1)}, s32[256]{0:T(256)}, u32[]{:S(2)}) copy-start(s32[256]{0:T(256)} %copy-done.59) | copy-start | bytes 3076
  329.5 27.2 %copy-start.70 = (pred[256]{0:T(512)(128)(4,1)S(1)}, pred[256]{0:T(512)(128)(4,1)}, u32[]{:S(2)}) copy-start(pred[256]{0:T(512)(128)(4,1)} %copy-done.69) | copy-start | bytes 772
  329.5 5.7 collective-permute-start.7
  330.6 28.5 %copy-start.62 = (f32[256]{0:T(256)S(1)}, f32[256]{0:T(256)}, u32[]{:S(2)}) copy-start(f32[256]{0:T(256)} %copy-done.61) | copy-start | bytes 3076
  330.6 28.5 %copy-start.54 = (s32[1,256,1]{1,2,0:T(1,128)S(1)}, s32[1,256,1]{1,2,0:T(1,128)}, u32[]{:S(2)}) copy-start(s32[1,256,1]{1,2,0:T(1,128)} %param.18) | copy-start | bytes 3076
  330.6 20.9 %all-to-all-start.2 = ((bf16[4,72,1024]{2,1,0:T(8,128)(2,1)}), bf16[4,72,1024]{2,1,0:T(8,128)(2,1)S(1)}, u32[]{:S(2)}, u32[]{:S(2)}) async-start(bf16[4,72,1024]{2,1,0:T(8,128)(2,1)} %bitcast.27), calls=%async_computation.2 | async-start | bytes 1179648 | tf_op jit(solution)/shard_map/all_to_all | solution.py:248
  335.1 37.1 %copy-start.5 = (f32[256,1024]{1,0:T(8,128)S(1)}, f32[256,1024]{1,0:T(8,128)}, u32[]{:S(2)}) copy-start(f32[256,1024]{1,0:T(8,128)} %copy-done.4) | copy-start | bytes 3145732
  335.1 37.1 %copy-start.48 = (f32[8,1,128]{2,1,0:T(1,128)S(1)}, f32[8,1,128]{2,1,0:T(1,128)}, u32[]{:S(2)}) copy-start(f32[8,1,128]{2,1,0:T(1,128)} %copy-done.47) | copy-start | bytes 12292
  335.1 37.1 %copy-start.52 = (f32[256]{0:T(256)S(1)}, f32[256]{0:T(256)}, u32[]{:S(2)}) copy-start(f32[256]{0:T(256)} %copy-done.51) | copy-start | bytes 3076
  335.1 37.1 %copy-start.58 = (f32[256]{0:T(256)S(1)}, f32[256]{0:T(256)}, u32[]{:S(2)}) copy-start(f32[256]{0:T(256)} %copy-done.57) | copy-start | bytes 3076
  338.2 36.3 %copy-start.66 = (f32[256]{0:T(256)S(1)}, f32[256]{0:T(256)}, u32[]{:S(2)}) copy-start(f32[256]{0:T(256)} %copy-done.65) | copy-start | bytes 3076
  338.2 36.4 %copy-start.68 = (f32[256]{0:T(256)S(1)}, f32[256]{0:T(256)}, u32[]{:S(2)}) copy-start(f32[256]{0:T(256)} %copy-done.67) | copy-start | bytes 3076
  352.4 19.8 %all-to-all-start.3 = ((bf16[4,72,1024]{2,1,0:T(8,128)(2,1)}), bf16[4,72,1024]{2,1,0:T(8,128)(2,1)}, u32[]{:S(2)}, u32[]{:S(2)}) async-start(bf16[4,72,1024]{2,1,0:T(8,128)(2,1)} %bitcast.31), calls=%async_computation.3 | async-start | bytes 1179648 | tf_op jit(solution)/shard_map/all_to_all | solution.py:248
  377.1 12.7 %copy-start.35 = (bf16[256,1024]{1,0:T(8,128)(2,1)}, bf16[256,1024]{1,0:T(8,128)(2,1)S(1)}, u32[]{:S(2)}) copy-start(bf16[256,1024]{1,0:T(8,128)(2,1)S(1)} %fusion.83) | copy-start | bytes 1572868
  378.6 11.8 %all-to-all-start.4 = ((bf16[256,4,256]{2,0,1:T(8,128)(2,1)}), bf16[256,4,256]{2,0,1:T(8,128)(2,1)}, u32[]{:S(2)}, u32[]{:S(2)}) async-start(bf16[256,4,256]{2,0,1:T(8,128)(2,1)} %bitcast.190), calls=%async_computation.4 | async-start | bytes 1048576 | tf_op jit(solution)/shard_map/all_to_all | solution.py:69
  382.8 109.3 %reduce-scatter.20.cloned.1.call-start = ((), (), s32[]{:S(2)}) async-start(), calls=%async_computation.21 | async-start | bytes 5242880 | tf_op jit(solution)/shard_map/reduce_scatter | solution.py:293
  389.8 107.6 %reduce-scatter.8.cloned.1.call-start = ((), (), s32[]{:S(2)}) async-start(), calls=%async_computation.14 | async-start | bytes 2621440 | tf_op jit(solution)/shard_map/reduce_scatter | solution.py:335
  462.7 90.6 %reduce-scatter.14.cloned.1.call-start = ((), (), s32[]{:S(2)}) async-start(), calls=%async_computation.18 | async-start | bytes 5242880 | tf_op jit(solution)/shard_map/reduce_scatter | solution.py:293
  469.6 136.1 %reduce-scatter.12.cloned.1.call-start = ((), (), s32[]{:S(2)}) async-start(), calls=%async_computation.16 | async-start | bytes 4718592 | tf_op jit(solution)/shard_map/reduce_scatter | solution.py:349
  473.6 186.1 %reduce-scatter.16.cloned.1.call-start = ((), (), s32[]{:S(2)}) async-start(), calls=%async_computation.19 | async-start | bytes 5242880 | tf_op jit(solution)/shard_map/reduce_scatter | solution.py:293
  481.9 220.4 %reduce-scatter.10.cloned.1.call-start = ((), (), s32[]{:S(2)}) async-start(), calls=%async_computation.15 | async-start | bytes 3538944 | tf_op jit(solution)/shard_map/reduce_scatter | solution.py:341
  488.5 10.3 %copy-start.64 = (f32[256]{0:T(256)S(1)}, f32[256]{0:T(256)}, u32[]{:S(2)}) copy-start(f32[256]{0:T(256)} %copy-done.63) | copy-start | bytes 3076
  488.5 10.3 %copy-start.56 = (f32[256]{0:T(256)S(1)}, f32[256]{0:T(256)}, u32[]{:S(2)}) copy-start(f32[256]{0:T(256)} %copy-done.55) | copy-start | bytes 3076
  488.5 260.7 %all-reduce.2.cloned.1.call-start = ((), (), s32[]{:S(2)}) async-start(), calls=%async_computation.17 | async-start | bytes 524288 | tf_op jit(solution)/shard_map/psum | solution.py:350
  489.1 52.4 %copy-start.12 = (f32[256,1024]{1,0:T(8,128)S(1)}, f32[256,1024]{1,0:T(8,128)}, u32[]{:S(2)}) copy-start(f32[256,1024]{1,0:T(8,128)} %copy-done.11) | copy-start | bytes 3145732
  489.2 52.4 %copy-start.15 = (bf16[1,256,1024]{2,1,0:T(8,128)(2,1)S(1)}, bf16[1,256,1024]{2,1,0:T(8,128)(2,1)}, u32[]{:S(2)}) copy-start(bf16[1,256,1024]{2,1,0:T(8,128)(2,1)} %param.29) | copy-start | bytes 1572868
  (47 other events, 180.2 us)
Sparse Core Ops, SparseCore 0:
  10.2 29.7 all-gather.13
  41.6 27.8 all-gather.15
  71.3 57.5 all-gather.17
  130.6 50.3 all-gather.19
  182.8 52.5 all-gather.21
  237.1 52.5 all-gather.23
  307.6 52.7 reduce-scatter.17
  389.9 52.0 reduce-scatter.19
  462.8 34.4 reduce-scatter.7
  500.2 53.0 reduce-scatter.13
  555.6 50.0 reduce-scatter.11
  608.5 51.0 reduce-scatter.15
  661.9 40.3 reduce-scatter.9
  705.7 43.4 all-reduce.1
